TPU v7x, 512 devices: a whole 4x4x16 slice. The times are simulated.
512 devices in a mesh: seq: 128 (over y, z, core), tp: 4 (over x).
Axes of the slice: x: 4, y: 4, z: 16, core: 2. Of those that a mesh axis runs over, the one named last changes fastest.
Arguments:
- queries: float32 [16384, 2048], P('seq', 'tp'), may hold values from -6 to 6
- keys: float32 [16384, 2048], P('seq', 'tp'), may hold values from -6 to 6
- values: float32 [16384, 2048], P('seq', 'tp'), may hold values from -6 to 6
- out_weight: float32 [2048, 4096], P('seq', 'tp'), may hold values from -0.125 to 0.125
Outputs:
- mixed: float32 [16384, 4096], P('seq', 'tp')
All inputs are finite; a program needn't handle non-finite values.
Results may differ from a plain program's by a relative error of at most 0.0003.
Values sent between devices are 32-bit elements; how exact they have to be, the bound alone decides.
A program may use at most 128 MiB of HBM per device.

v0:
```python
import jax
import jax.numpy as jnp
from jax import lax
from jax.sharding import PartitionSpec as P

DH = 128


def prefix(part, axis, combine, identity):
    place = lax.axis_index(axis)
    gathered = jax.tree.map(lambda a: lax.all_gather(a, axis), part)
    state = jax.tree.map(lambda a, e: jnp.zeros_like(a) + jnp.asarray(e, a.dtype), part, identity)

    def one(step, state):
        return combine(
            state, jax.tree.map(lambda a: lax.dynamic_index_in_dim(a, step, 0, False), gathered)
        )

    return lax.fori_loop(0, place, one, state)


def features(inputs):
    return jnp.where(inputs > 0, inputs + 1.0, jnp.exp(jnp.minimum(inputs, 0.0)))


def combine(earlier, later):
    return (earlier[0] + later[0], earlier[1] + later[1])


def shards(queries, keys, values, out_weight):
    highest = lax.Precision.HIGHEST
    tok_rows = queries.shape[0]
    heads_here = queries.shape[1] // DH
    phi_queries = features(queries).reshape(tok_rows, heads_here, DH)
    phi_keys = features(keys).reshape(tok_rows, heads_here, DH)
    value_heads = values.reshape(tok_rows, heads_here, DH)
    memory_state = jnp.einsum("shd,she->hde", phi_keys, value_heads, precision=highest)
    key_total = jnp.sum(phi_keys, axis=0)
    identity = (jnp.zeros_like(memory_state), jnp.zeros_like(key_total))
    prior_state, prior_total = prefix((memory_state, key_total), "seq", combine, identity)
    causal_mask = jnp.arange(tok_rows)[:, None] >= jnp.arange(tok_rows)[None, :]
    scores = jnp.einsum("thd,shd->hts", phi_queries, phi_keys, precision=highest)
    scores = jnp.where(causal_mask[None], scores, 0.0)
    numerator = jnp.einsum("hts,shd->thd", scores, value_heads, precision=highest)
    numerator = numerator + jnp.einsum("thd,hde->the", phi_queries, prior_state, precision=highest)
    denominator = jnp.sum(scores, axis=2).T + jnp.einsum(
        "thd,hd->th", phi_queries, prior_total, precision=highest
    )
    attended = (numerator / denominator[:, :, None]).reshape(tok_rows, heads_here * DH)
    every_head = lax.all_gather(attended, "tp", axis=1, tiled=True)
    gathered = lax.all_gather(out_weight, "seq", axis=0, tiled=True)
    mixed = jnp.dot(every_head, gathered, precision=highest, preferred_element_type=jnp.float32)
    return mixed


def solution(mesh):
    return jax.shard_map(
        shards,
        mesh=mesh,
        in_specs=(P("seq", "tp"), P("seq", "tp"), P("seq", "tp"), P("seq", "tp")),
        out_specs=P("seq", "tp"),
        check_vma=False,
    )
```

profile of v0, /device:TPU:1, one launch (start us, length us, event | category | flops | bytes accessed | tf_op | source)
XLA Modules:
  0.0 401.2 jit_solution(6245858117362999715)
XLA Ops:
  6.5 0.0 copy-start
  6.5 0.0 all-gather.9.cloned.1.call-start
  6.5 1.1 fusion.7
  7.6 0.1 copy.31
  7.7 0.0 copy-done
  7.8 1.1 fusion.3
  8.8 0.0 all-gather.9.cloned.1.call-update
  8.9 0.0 all-gather.7.cloned.1.call-start
  8.9 0.7 all-gather.7.cloned.1.call-update
  9.6 0.0 all-gather.5.cloned.1.call-start
  9.7 1.0 exponential_select_fusion.1
  10.7 0.1 copy.30
  10.8 108.5 %all_gather.21 = f32[128,4,128]{2,1,0:T(4,128)S(1)} all-gather(f32[1,4,128]{2,1,0:T(4,128)S(1)} %bitcast.58), channel_id=1, replica_groups=mesh['seq'=128,'tp'=4] {'seq'}, dimensions={0}, use_global_device_ids=true | all-gather | bytes 264192 | tf_op jit(solution)/shard_map/all_gather | solution.py:11
  119.4 0.6 fusion.8
  120.0 0.6 convolution_bitcast_fusion.1
  120.6 90.9 %all-gather.9.cloned.1.call-done = f32[512,128,128]{2,1,0:T(8,128)} async-done(((f32[4,128,128]{2,1,0:T(8,128)}), f32[512,128,128]{2,1,0:T(8,128)}) %all-gather.9.cloned.1.call-update) | async-done | bytes 33554448 | tf_op jit(solution)/shard_map/all_gather | solution.py:11
  211.6 1.1 while.12
  211.6 1.0 bitcast_add_fusion.4
  212.6 0.3 fusion.9
  212.9 1.3 fusion.1
  214.3 0.0 all-gather.5.cloned.1.call-update
  214.3 143.7 %all-gather.7.cloned.1.call-done = f32[2048,1024]{1,0:T(8,128)} async-done(((f32[16,1024]{1,0:T(8,128)}), f32[2048,1024]{1,0:T(8,128)}) %all-gather.7.cloned.1.call-update) | async-done | bytes 8388624 | tf_op jit(solution)/shard_map/all_gather | solution.py:51
  358.0 27.5 %all-gather.5.cloned.1.call-done = f32[128,2048]{0,1:T(8,128)} async-done(((f32[128,512]{0,1:T(8,128)}), f32[128,2048]{0,1:T(8,128)}) %all-gather.5.cloned.1.call-update) | async-done | bytes 1048592 | tf_op jit(solution)/shard_map/all_gather | solution.py:50
  385.5 9.1 %fusion.10 = f32[128,1024]{1,0:T(8,128)} fusion(f32[128,2048]{0,1:T(8,128)} %all-gather.5.cloned.1.call-done, f32[2048,1024]{1,0:T(8,128)} %all-gather.7.cloned.1.call-done), kind=kOutput, calls=%fused_computation.19 | convolution fusion | flops 3221225472 | bytes 9961472 | tf_op jit(solution)/shard_map/dot_general | solution.py:52
  (5 shorter events, 0.1 us)
Async XLA Ops:
  6.5 1.2 copy-start
  6.5 205.0 %all-gather.9.cloned.1.call-start = ((), (), s32[]{:S(2)}) async-start(), calls=%async_computation.2 | async-start | bytes 33816576 | tf_op jit(solution)/shard_map/all_gather | solution.py:11
  8.9 349.1 %all-gather.7.cloned.1.call-start = ((), (), s32[]{:S(2)}) async-start(), calls=%async_computation.1 | async-start | bytes 8454144 | tf_op jit(solution)/shard_map/all_gather | solution.py:51
  9.6 375.9 %all-gather.5.cloned.1.call-start = ((), (), s32[]{:S(2)}) async-start(), calls=%async_computation | async-start | bytes 1310720 | tf_op jit(solution)/shard_map/all_gather | solution.py:50
Sparse Core Ops, SparseCore 0:
  10.5 200.9 all-gather.8
  214.7 143.2 all-gather.6
  360.1 25.3 all-gather.4
where the time goes:
time: 405 us; the launch traced here: 401 us
  waiting for transfers between devices  263 us (65%)
  blocking collectives  109 us (27%)
  between operations  13.2 us (3%)
  matrix products  13.1 us (3%)
    all_gather x1, waiting for transfers between devices, shards(): gathered = lax.all_gather(out_weight, 'seq', axis=0, tiled=True)  144 us
    all_gather x1, blocking collectives, prefix(): gathered = jax.tree.map(lambda a: lax.all_gather(a, axis), part)  109 us
    all_gather x1, waiting for transfers between devices, prefix(): gathered = jax.tree.map(lambda a: lax.all_gather(a, axis), part)  90.9 us
    all_gather x1, waiting for transfers between devices, shards(): every_head = lax.all_gather(attended, 'tp', axis=1, tiled=True)  27.5 us
    dot_general x1, matrix products, shards(): jnp.dot(every_head, gathered, precision=highest, preferred_element_type=j...  9.14 us
  transfers between devices with their start and end apart: 3, of which 3 were waited for; matrix products, arithmetic and copies ran while one was open for 1% of the time, Pallas kernels for 0%

commit v1 on v0

--- a/solution.py
+++ b/solution.py
@@ -48,7 +48,9 @@
     )
     attended = (numerator / denominator[:, :, None]).reshape(tok_rows, heads_here * DH)
     every_head = lax.all_gather(attended, "tp", axis=1, tiled=True)
-    gathered = lax.all_gather(out_weight, "seq", axis=0, tiled=True)
+    gathered = jnp.concatenate(
+        lax.all_to_all(jnp.stack([out_weight] * lax.axis_size("seq")), "seq", 0, 0), axis=0
+    )
     mixed = jnp.dot(every_head, gathered, precision=highest, preferred_element_type=jnp.float32)
     return mixed
 

time: 405 us -> 752 us (1.86)
  blocking collectives: 109 us -> 538 us
  waiting for transfers between devices: 263 us -> 154 us
  starting transfers between devices: 0.08 us -> 21.2 us
    all_gather x1, blocking collectives: 109 us -> 538 us  [prefix(): gathered = jax.tree.map(lambda a: lax.all_gather(a, axis), part)]
    all_gather x1 -> x0, waiting for transfers between devices: 144 us -> none  [shards(): gathered = lax.all_gather(out_weight, 'seq', axis=0, tiled=True)]
    all_gather x1, waiting for transfers between devices: 27.5 us -> 154 us  [shards(): every_head = lax.all_gather(attended, 'tp', axis=1, tiled=True)]
    all_gather x1, waiting for transfers between devices: 90.9 us -> 0.02 us  [prefix(): gathered = jax.tree.map(lambda a: lax.all_gather(a, axis), part)]
    all_to_all x0 -> x1, starting transfers between devices: none -> 21.2 us  [shards(): lax.all_to_all(jnp.stack([out_weight] * lax.axis_size('seq')), 'seq', 0, 0)]
  transfers between devices with their start and end apart: 3 -> 3, of which waited for: 3 -> 1; matrix products, arithmetic and copies ran while one was open for 1% -> 1% of each run, Pallas kernels for 0% -> 0%
where the time goes in v1:
time: 752 us; the launch traced here: 747 us
  blocking collectives  538 us (72%)
  waiting for transfers between devices  154 us (20%)
  starting transfers between devices  21.2 us (3%)
  between operations  13.5 us (2%)
  matrix products  13.1 us (2%)
    all_gather x1, blocking collectives, prefix(): gathered = jax.tree.map(lambda a: lax.all_gather(a, axis), part)  538 us
    all_gather x1, waiting for transfers between devices, shards(): every_head = lax.all_gather(attended, 'tp', axis=1, tiled=True)  154 us
    all_to_all x1, starting transfers between devices, shards(): lax.all_to_all(jnp.stack([out_weight] * lax.axis_size('seq')), 'seq', 0, 0)  21.2 us
  transfers between devices with their start and end apart: 3, of which 1 were waited for; matrix products, arithmetic and copies ran while one was open for 1% of the time, Pallas kernels for 0%

profile of v1, /device:TPU:1, one launch (start us, length us, event | category | flops | bytes accessed | tf_op | source)
XLA Modules:
  0.0 747.4 jit_solution(8074428069715510336)
XLA Ops:
  6.5 0.0 copy-start
  6.5 0.0 all-gather.6.cloned.1.call-start
  6.5 1.1 fusion.7
  7.6 0.1 copy.31
  7.7 0.0 copy-done
  7.8 1.1 fusion.3
  8.8 0.0 all-gather.6.cloned.1.call-update
  8.9 5.1 stack.2
  14.0 0.0 copy-start.1
  14.0 21.2 %all-to-all-start = ((f32[128,16,1024]{2,1,0:T(8,128)}), f32[128,16,1024]{2,1,0:T(8,128)}, u32[]{:S(2)}, u32[]{:S(2)}) async-start(f32[128,16,1024]{2,1,0:T(8,128)} %stack.2), calls=%async_computation | async-start | bytes 16777216 | tf_op jit(solution)/shard_map/all_to_all | solution.py:52
  35.1 0.0 all-gather.4.cloned.1.call-start
  35.2 0.0 copy-done.1
  35.2 0.1 exponential_select_fusion.1
  35.3 0.1 copy.30
  35.4 537.6 %all_gather.18 = f32[128,4,128]{2,1,0:T(4,128)S(1)} all-gather(f32[1,4,128]{2,1,0:T(4,128)S(1)} %bitcast.59), channel_id=1, replica_groups=mesh['seq'=128,'tp'=4] {'seq'}, dimensions={0}, use_global_device_ids=true | all-gather | bytes 264192 | tf_op jit(solution)/shard_map/all_gather | solution.py:11
  573.0 0.6 fusion.8
  573.6 0.6 convolution_bitcast_fusion.1
  574.2 0.0 all-gather.6.cloned.1.call-done
  574.3 1.1 while.12
  574.3 1.0 bitcast_add_fusion.4
  575.4 0.3 fusion.9
  575.7 1.3 fusion.1
  577.0 0.0 all-gather.4.cloned.1.call-update
  577.0 0.0 all-to-all-done
  577.0 154.4 %all-gather.4.cloned.1.call-done = f32[128,2048]{0,1:T(8,128)} async-done(((f32[128,512]{0,1:T(8,128)}), f32[128,2048]{0,1:T(8,128)}) %all-gather.4.cloned.1.call-update) | async-done | bytes 1048592 | tf_op jit(solution)/shard_map/all_gather | solution.py:50
  731.4 9.1 %fusion.10 = f32[128,1024]{1,0:T(8,128)} fusion(f32[128,2048]{0,1:T(8,128)} %all-gather.4.cloned.1.call-done, f32[2048,1024]{1,0:T(8,128)} %bitcast.12), kind=kOutput, calls=%fused_computation.19 | convolution fusion | flops 3221225472 | bytes 9961472 | tf_op jit(solution)/shard_map/dot_general | solution.py:54
  (5 shorter events, 0.1 us)
Async XLA Ops:
  6.5 1.2 copy-start
  6.5 567.7 %all-gather.6.cloned.1.call-start = ((), (), s32[]{:S(2)}) async-start(), calls=%async_computation.2 | async-start | bytes 33816576 | tf_op jit(solution)/shard_map/all_gather | solution.py:11
  14.0 21.2 %copy-start.1 = (f32[128,512]{1,0:T(8,128)S(1)}, f32[128,512]{1,0:T(8,128)}, u32[]{:S(2)}) copy-start(f32[128,512]{1,0:T(8,128)} %param.6) | copy-start | bytes 786436
  14.0 563.0 %all-to-all-start = ((f32[128,16,1024]{2,1,0:T(8,128)}), f32[128,16,1024]{2,1,0:T(8,128)}, u32[]{:S(2)}, u32[]{:S(2)}) async-start(f32[128,16,1024]{2,1,0:T(8,128)} %stack.2), calls=%async_computation | async-start | bytes 16777216 | tf_op jit(solution)/shard_map/all_to_all | solution.py:52
  35.1 696.2 %all-gather.4.cloned.1.call-start = ((), (), s32[]{:S(2)}) async-start(), calls=%async_computation.1 | async-start | bytes 1310720 | tf_op jit(solution)/shard_map/all_gather | solution.py:50
Sparse Core Ops, SparseCore 0:
  10.5 494.6 all-gather.5
  577.1 154.1 all-gather.3

commit v2 on v0

--- a/solution.py
+++ b/solution.py
@@ -47,7 +47,26 @@
         "thd,hd->th", phi_queries, prior_total, precision=highest
     )
     attended = (numerator / denominator[:, :, None]).reshape(tok_rows, heads_here * DH)
-    every_head = lax.all_gather(attended, "tp", axis=1, tiled=True)
+    devices, index, rows = (lax.axis_size("tp"), lax.axis_index("tp"), attended.shape[1])
+    upward = [(i, (i + 1) % devices) for i in range(devices)]
+    left = [(i, (i - 1) % devices) for i in range(devices)]
+    result = jnp.zeros(
+        (*attended.shape[:1], devices * rows, *attended.shape[1 + 1 :]), attended.dtype
+    )
+    result = lax.dynamic_update_slice_in_dim(result, attended, index * rows, axis=1)
+    from_left = from_right = attended
+    middle = devices // 2
+    for hop in range(1, middle + 1):
+        from_left = lax.ppermute(from_left, "tp", upward)
+        result = lax.dynamic_update_slice_in_dim(
+            result, from_left, (index - hop) % devices * rows, axis=1
+        )
+        if hop < devices - middle:
+            from_right = lax.ppermute(from_right, "tp", left)
+            result = lax.dynamic_update_slice_in_dim(
+                result, from_right, (index + hop) % devices * rows, axis=1
+            )
+    every_head = result
     gathered = lax.all_gather(out_weight, "seq", axis=0, tiled=True)
     mixed = jnp.dot(every_head, gathered, precision=highest, preferred_element_type=jnp.float32)
     return mixed

time: 405 us -> 377 us (0.931)
  waiting for transfers between devices: 263 us -> 227 us
  starting transfers between devices: 0.08 us -> 8.71 us
    all_gather x1 -> x0, waiting for transfers between devices: 27.5 us -> none  [shards(): every_head = lax.all_gather(attended, 'tp', axis=1, tiled=True)]
    all_gather x1, waiting for transfers between devices: 144 us -> 123 us  [shards(): gathered = lax.all_gather(out_weight, 'seq', axis=0, tiled=True)]
    ppermute x0 -> x3, waiting for transfers between devices: none -> 12.5 us  [the longest x2 12.4 us: shards(): from_left = lax.ppermute(from_left, 'tp', upward)]
    ppermute x0 -> x3, starting transfers between devices: none -> 8.66 us  [the longest x2 5.27 us: shards(): from_left = lax.ppermute(from_left, 'tp', upward)]
  transfers between devices with their start and end apart: 3 -> 5, of which waited for: 3 -> 5; matrix products, arithmetic and copies ran while one was open for 1% -> 1% of each run, Pallas kernels for 0% -> 0%
where the time goes in v2:
time: 377 us; the launch traced here: 373 us
  waiting for transfers between devices  227 us (60%)
  blocking collectives  109 us (29%)
  between operations  13.6 us (4%)
  matrix products  11 us (3%)
  starting transfers between devices  8.71 us (2%)
    all_gather x1, waiting for transfers between devices, shards(): gathered = lax.all_gather(out_weight, 'seq', axis=0, tiled=True)  123 us
    all_gather x1, blocking collectives, prefix(): gathered = jax.tree.map(lambda a: lax.all_gather(a, axis), part)  109 us
    all_gather x1, waiting for transfers between devices, prefix(): gathered = jax.tree.map(lambda a: lax.all_gather(a, axis), part)  91.2 us
    ppermute x2, waiting for transfers between devices, shards(): from_left = lax.ppermute(from_left, 'tp', upward)  12.4 us
    dot_general x1, matrix products, shards(): jnp.dot(every_head, gathered, precision=highest, preferred_element_type=j...  7.79 us
  transfers between devices with their start and end apart: 5, of which 5 were waited for; matrix products, arithmetic and copies ran while one was open for 1% of the time, Pallas kernels for 0%

profile of v2, /device:TPU:1, one launch (start us, length us, event | category | flops | bytes accessed | tf_op | source)
XLA Modules:
  0.0 372.9 jit_solution(12443284118268577519)
XLA Ops:
  6.5 0.0 copy-start
  6.5 0.0 all-gather.6.cloned.1.call-start
  6.5 1.1 fusion.7
  7.6 0.1 copy.31
  7.7 0.0 copy-done
  7.8 1.1 fusion.3
  8.8 0.0 all-gather.6.cloned.1.call-update
  8.9 0.0 all-gather.4.cloned.1.call-start
  8.9 0.7 all-gather.4.cloned.1.call-update
  9.6 1.0 exponential_select_fusion.1
  10.6 0.1 copy.30
  10.8 108.6 %all_gather.18 = f32[128,4,128]{2,1,0:T(4,128)S(1)} all-gather(f32[1,4,128]{2,1,0:T(4,128)S(1)} %bitcast.60), channel_id=1, replica_groups=mesh['seq'=128,'tp'=4] {'seq'}, dimensions={0}, use_global_device_ids=true | all-gather | bytes 264192 | tf_op jit(solution)/shard_map/all_gather | solution.py:11
  119.3 0.6 fusion.8
  120.0 0.6 convolution_bitcast_fusion.1
  120.6 91.2 %all-gather.6.cloned.1.call-done = f32[512,128,128]{2,1,0:T(8,128)} async-done(((f32[4,128,128]{2,1,0:T(8,128)}), f32[512,128,128]{2,1,0:T(8,128)}) %all-gather.6.cloned.1.call-update) | async-done | bytes 33554448 | tf_op jit(solution)/shard_map/all_gather | solution.py:11
  211.8 1.1 while.12
  211.8 1.0 bitcast_add_fusion.4
  212.9 0.3 fusion.9
  213.2 0.6 fusion.1
  213.8 3.1 collective-permute-start
  216.9 3.4 collective-permute-start.1
  220.4 4.2 %collective-permute-done = f32[128,512]{0,1:T(8,128)S(1)} collective-permute-done((f32[128,512]{0,1:T(8,128)S(1)}, f32[128,512]{0,1:T(8,128)S(1)}, u32[]{:S(2)}, u32[]{:S(2)}) %collective-permute-start) | collective-permute-done | bytes 262176 | tf_op jit(solution)/shard_map/ppermute | solution.py:60
  224.6 2.2 collective-permute-start.2
  226.8 0.1 broadcast_in_dim.23
  226.9 0.1 collective-permute-done.1
  227.0 8.2 %collective-permute-done.2 = f32[128,512]{0,1:T(8,128)S(1)} collective-permute-done((f32[128,512]{0,1:T(8,128)S(1)}, f32[128,512]{0,1:T(8,128)S(1)}, u32[]{:S(2)}, u32[]{:S(2)}) %collective-permute-start.2) | collective-permute-done | bytes 262176 | tf_op jit(solution)/shard_map/ppermute | solution.py:60
  235.3 123.0 %all-gather.4.cloned.1.call-done = f32[2048,1024]{1,0:T(8,128)} async-done(((f32[16,1024]{1,0:T(8,128)}), f32[2048,1024]{1,0:T(8,128)}) %all-gather.4.cloned.1.call-update) | async-done | bytes 8388624 | tf_op jit(solution)/shard_map/all_gather | solution.py:70
  358.3 7.8 %fusion.10 = f32[128,1024]{1,0:T(8,128)} fusion(f32[128,2048]{0,1:T(8,128)S(1)} %constant_dynamic-update-slice_fusion, f32[2048,1024]{1,0:T(8,128)} %all-gather.4.cloned.1.call-done), kind=kOutput, calls=%fused_computation.23 | convolution fusion | flops 3221225472 | bytes 9961472 | tf_op jit(solution)/shard_map/dot_general | solution.py:71
  (9 shorter events, 0.2 us)
Async XLA Ops:
  6.5 1.2 copy-start
  6.5 205.2 %all-gather.6.cloned.1.call-start = ((), (), s32[]{:S(2)}) async-start(), calls=%async_computation.1 | async-start | bytes 33816576 | tf_op jit(solution)/shard_map/all_gather | solution.py:11
  8.9 349.4 %all-gather.4.cloned.1.call-start = ((), (), s32[]{:S(2)}) async-start(), calls=%async_computation | async-start | bytes 8454144 | tf_op jit(solution)/shard_map/all_gather | solution.py:70
  213.8 10.8 %collective-permute-start = (f32[128,512]{0,1:T(8,128)S(1)}, f32[128,512]{0,1:T(8,128)S(1)}, u32[]{:S(2)}, u32[]{:S(2)}) collective-permute-start(f32[128,512]{0,1:T(8,128)S(1)} %bitcast.55), channel_id=1, source_target_pairs={{0,1},{1,2},{2,3},{3,0},{4,5},{5,6},{6,7},{7,4},{8,9},{9,10},{10,1... | collective-permute-start | bytes 786440 | tf_op jit(solution)/shard_map/ppermute | solution.py:60
  216.9 10.1 %collective-permute-start.1 = (f32[128,512]{0,1:T(8,128)S(1)}, f32[128,512]{0,1:T(8,128)S(1)}, u32[]{:S(2)}, u32[]{:S(2)}) collective-permute-start(f32[128,512]{0,1:T(8,128)S(1)} %bitcast.56), channel_id=1, source_target_pairs={{0,3},{1,0},{2,1},{3,2},{4,7},{5,4},{6,5},{7,6},{8,11},{9,8},{10,9... | collective-permute-start | bytes 786440 | tf_op jit(solution)/shard_map/ppermute | solution.py:65
  224.6 10.6 %collective-permute-start.2 = (f32[128,512]{0,1:T(8,128)S(1)}, f32[128,512]{0,1:T(8,128)S(1)}, u32[]{:S(2)}, u32[]{:S(2)}) collective-permute-start(f32[128,512]{0,1:T(8,128)S(1)} %collective-permute-done), channel_id=1, source_target_pairs={{0,1},{1,2},{2,3},{3,0},{4,5},{5,6},{6,7},{7,4},{8,9},{9,10},{10,1... | collective-permute-start | bytes 786440 | tf_op jit(solution)/shard_map/ppermute | solution.py:60
Sparse Core Ops, SparseCore 0:
  10.5 201.2 all-gather.5
  214.9 143.2 all-gather.3
